TPU v7x, 512 devices: a whole 4x8x8 slice. The times are simulated.
512 devices in a mesh: bead: 32 (over z, x_hi, core), space: 16 (over y, x_lo).
Axes of the slice: x: 4 (x_hi: 2, x_lo: 2; x = x_hi * 2 + x_lo), y: 8, z: 8, core: 2. Of those that a mesh axis runs over, the one named last changes fastest.
Arguments:
- positions: float32 [3, 32, 65536], P(None, 'bead', 'space'), may hold values from -0.12 to 2.12
- momenta: float32 [3, 32, 65536], P(None, 'bead', 'space'), may hold values from -6 to 6
- atom_types: int32 [65536], P('space'), may hold values from 0 to 3
- neighbours: int32 [512, 5], P('space'), may hold values from 0 to 511, as said below
- thermal_noise: float32 [2, 3, 32, 65536], P(None, None, 'bead', 'space'), may hold values from -6 to 6
Outputs:
- positions_out: float32 [3, 32, 65536], P(None, 'bead', 'space')
- momenta_out: float32 [3, 32, 65536], P(None, 'bead', 'space')
Inputs may be any that keep to these rules, and one draw needn't show every extreme that they name: `neighbours`: the row of block b holds 5 different blocks within 4 blocks of b, b itself and one block exactly 4 away among them.
All inputs are finite; a program needn't handle non-finite values.
Results may differ from a plain program's by a relative error of at most 0.0003.
Values sent between devices are 32-bit elements; how exact they have to be, the bound alone decides.
A program may use at most 64 MiB of HBM per device.

v0:
```python
import math

import jax
import jax.numpy as jnp
from jax import lax
from jax.sharding import PartitionSpec as P

BEADS = 32
BLOCK = 128
HALO = 4


half_step = 0.025
time_step = 0.05
chain_freq = 12.0
thermal = 0.375
centroid_friction = 1.0
screening = 4.0
softening = 0.09
highest = lax.Precision.HIGHEST


def padded(cells, sides, width):
    for axis, dim in sides:
        count = lax.axis_size(axis)
        ends = count - 1
        head = lax.slice_in_dim(cells, 0, width, axis=dim)
        tail = lax.slice_in_dim(cells, cells.shape[dim] - width, cells.shape[dim], axis=dim)
        cells = jnp.concatenate(
            [
                lax.ppermute(tail, axis, [(i, (i + 1) % count) for i in range(ends)]),
                cells,
                lax.ppermute(head, axis, [((i + 1) % count, i) for i in range(ends)]),
            ],
            axis=dim,
        )
    return cells


def materials(atom_types):
    onehot = (atom_types[:, None] == jnp.arange(4, dtype=jnp.int32)[None, :]).astype(jnp.float32)
    charge_table = jnp.array([1.0, -1.0, 0.6, -1.4], dtype=jnp.float32)
    mass_table = jnp.array([1.0, 2.0, 3.0, 4.0], dtype=jnp.float32)
    return (
        jnp.sum(onehot * charge_table[None, :], axis=1),
        jnp.sum(onehot * mass_table[None, :], axis=1),
    )


def mode_matrix(bead_total):
    bead_ids = jnp.arange(bead_total, dtype=jnp.float32)[:, None]
    mode_ids = jnp.arange(bead_total, dtype=jnp.int32)[None, :]
    phase_grid = 2.0 * jnp.pi * bead_ids * mode_ids.astype(jnp.float32) / bead_total
    half_mode = bead_total // 2
    plain = 1.0 / math.sqrt(bead_total)
    paired = math.sqrt(2.0 / bead_total)
    return jnp.where(
        mode_ids == 0,
        plain + 0.0 * phase_grid,
        jnp.where(
            mode_ids < half_mode,
            paired * jnp.cos(phase_grid),
            jnp.where(
                mode_ids == half_mode, plain * jnp.cos(phase_grid), paired * jnp.sin(phase_grid)
            ),
        ),
    )


def mode_tables(bead_total):
    mode_ids = jnp.arange(bead_total, dtype=jnp.float32)
    frequency = 2.0 * chain_freq * jnp.sin(jnp.pi * mode_ids / bead_total)
    angle_step = frequency * time_step
    cosine = jnp.cos(angle_step)
    sine_ratio = jnp.where(
        mode_ids == 0, time_step, jnp.sin(angle_step) / jnp.where(mode_ids == 0, 1.0, frequency)
    )
    stiffness = frequency * jnp.sin(angle_step)
    friction = jnp.where(mode_ids == 0, centroid_friction, 2.0 * frequency)
    damping = jnp.exp(-friction * time_step)
    kick_scale = jnp.sqrt(1.0 - damping * damping)
    return (cosine, sine_ratio, stiffness, damping, kick_scale)


def tile_force(own_rows, tile_rows, shift_rows):
    delta_x = (
        own_rows[0][:, None, :, None] - tile_rows[0][:, :, None, :] + shift_rows[:, :, None, None]
    )
    delta_y = own_rows[1][:, None, :, None] - tile_rows[1][:, :, None, :]
    delta_z = own_rows[2][:, None, :, None] - tile_rows[2][:, :, None, :]
    square = delta_x * delta_x + delta_y * delta_y + delta_z * delta_z + softening
    distance = jnp.sqrt(square)
    weight = (
        jnp.exp(-distance / screening) * (1.0 / (screening * distance) + 1.0 / square) / distance
    )
    weight = weight * tile_rows[3][:, :, None, :]
    force_x = own_rows[3] * jnp.sum(weight * delta_x, axis=(1, 3))
    force_y = own_rows[3] * jnp.sum(weight * delta_y, axis=(1, 3))
    force_z = own_rows[3] * jnp.sum(weight * delta_z, axis=(1, 3))
    return jnp.stack([force_x, force_y, force_z])


def bead_forces(extended, first_block, lists, offsets, group_size):
    block_count = lists.shape[0]

    def group_force(group_index):
        begin_row = group_index * group_size
        own_rows = lax.dynamic_slice_in_dim(extended, first_block + begin_row, group_size, 1)
        list_rows = lax.dynamic_slice_in_dim(lists, begin_row, group_size, 0)
        shift_rows = lax.dynamic_slice_in_dim(offsets, begin_row, group_size, 0)
        tile_rows = jnp.take(extended, list_rows, axis=1)
        return tile_force(own_rows, tile_rows, shift_rows)

    result = lax.map(group_force, jnp.arange(block_count // group_size, dtype=jnp.int32))
    return jnp.transpose(result, (1, 0, 2, 3)).reshape(3, block_count * extended.shape[2])


def thermostat_and_drift(mode_coords, mode_moment, noise_now, atom_mass, tables):
    cosine, sine_ratio, stiffness, damping, kick_scale = tuple(
        (entry[None, :, None] for entry in tables)
    )
    mass_row = atom_mass[None, None, :]
    moment_new = damping * mode_moment + kick_scale * jnp.sqrt(thermal * mass_row) * noise_now
    next_coords = cosine * mode_coords + sine_ratio * moment_new / mass_row
    next_moment = cosine * moment_new - stiffness * mass_row * mode_coords
    return (next_coords, next_moment)


def body(positions, momenta, atom_types, neighbours, thermal_noise):
    bead_count = positions.shape[1]
    atom_count = positions.shape[2]
    block_count = atom_count // BLOCK
    charge, atom_mass = materials(atom_types)
    matrix = mode_matrix(BEADS)
    tables = mode_tables(BEADS)
    first_block = lax.axis_index("space") * block_count
    own_blocks = first_block + jnp.arange(block_count, dtype=jnp.int32)
    offsets = (own_blocks[:, None] - neighbours).astype(jnp.float32)
    local_lists = neighbours - first_block + HALO
    charge_rows = charge[None, None, :]
    bead_start = lax.axis_index("bead") * bead_count

    def forces(coords):
        packed = jnp.concatenate([coords, charge_rows], axis=0)
        widened = padded(packed, (("space", 2),), HALO * BLOCK)
        extended = widened.reshape(4, bead_count, block_count + 2 * HALO, BLOCK)

        def one_bead(single):
            return bead_forces(single, HALO, local_lists, offsets, 2)

        return jax.vmap(one_bead, in_axes=1, out_axes=1)(extended)

    forces_now = forces(positions)
    coords, moment = (positions, momenta)
    for turn_index in range(thermal_noise.shape[0]):
        moment = moment + half_step * forces_now
        noise_now = thermal_noise[turn_index]
        local_tables = tuple(
            (lax.dynamic_slice_in_dim(entry, bead_start, bead_count) for entry in tables)
        )
        pieces = (
            lax.all_gather(coords, "bead", axis=1, tiled=True),
            lax.all_gather(moment, "bead", axis=1, tiled=True),
        )
        part_matrix = lax.dynamic_slice(matrix, (0, bead_start), (pieces[0].shape[1], bead_count))
        mode_coords = jnp.einsum("jk,cja->cka", part_matrix, pieces[0], precision=highest)
        mode_moment = jnp.einsum("jk,cja->cka", part_matrix, pieces[1], precision=highest)
        next_coords, next_moment = thermostat_and_drift(
            mode_coords, mode_moment, noise_now, atom_mass, local_tables
        )
        to_pieces = (
            lax.all_gather(next_coords, "bead", axis=1, tiled=True),
            lax.all_gather(next_moment, "bead", axis=1, tiled=True),
        )
        to_part_matrix = lax.dynamic_slice(
            matrix, (bead_start, 0), (bead_count, to_pieces[0].shape[1])
        )
        coords = jnp.einsum("jk,cka->cja", to_part_matrix, to_pieces[0], precision=highest)
        moment = jnp.einsum("jk,cka->cja", to_part_matrix, to_pieces[1], precision=highest)
        forces_now = forces(coords)
        moment = moment + half_step * forces_now
    return (coords, moment)


def solution(mesh):
    placed = (
        P(None, "bead", "space"),
        P(None, "bead", "space"),
        P("space"),
        P("space", None),
        P(None, None, "bead", "space"),
    )
    return jax.shard_map(
        body,
        mesh=mesh,
        in_specs=placed,
        out_specs=(P(None, "bead", "space"), P(None, "bead", "space")),
        check_vma=False,
    )
```

profile of v0, /device:TPU:1, one launch (start us, length us, event | category | flops | bytes accessed | tf_op | source)
XLA Modules:
  0.0 813.2 jit_solution(5201067347075179017)
XLA Ops:
  7.2 1.5 copy.135
  10.4 1.3 collective-permute-start.1
  11.7 4.6 collective-permute-start
  18.1 85.5 %while.39 = (s32[]{:T(128)}, f32[16,1,3,2,128]{4,3,2,1,0:T(2,128)S(1)}, s32[16]{0:T(128)S(1)}, f32[1,4,40,128]{3,1,2,0:T(4,128)S(1)}, s32[32,5]{1,0:T(8,128)S(1)...) while((s32[]{:T(128)}, ...), condition=%wide.region_5.7_spmd, body=%wide.region_1.6_spmd.sunk | while | flops 4103759 | bytes 419553 | solution.py:114
  42.9 1.2 multiply_reduce_fusion.6
  48.3 1.2 multiply_reduce_fusion.6
  53.6 1.2 multiply_reduce_fusion.6
  80.3 1.2 multiply_reduce_fusion.6
  101.7 1.2 multiply_reduce_fusion.6
  108.2 1.3 broadcast_multiply_fusion
  109.6 3.2 fusion.53
  112.9 87.3 %all-gather.17.cloned.1.call-done = f32[3,32,4096]{2,0,1:T(4,128)} async-done(((f32[3,1,4096]{2,0,1:T(4,128)}), f32[3,32,4096]{2,0,1:T(4,128)}) %all-gather.17.cloned.1.call-update) | async-done | bytes 1572880 | tf_op jit(solution)/shard_map/all_gather | solution.py:163
  200.1 3.3 fusion.51
  203.4 2.7 fusion.59
  206.8 81.7 %all-gather.19.cloned.1.call-done = f32[3,131072]{1,0:T(4,128)} async-done(((f32[3,4096]{1,0:T(4,128)}), f32[3,131072]{1,0:T(4,128)}) %all-gather.19.cloned.1.call-update) | async-done | bytes 1572880 | tf_op jit(solution)/shard_map/all_gather | solution.py:172
  288.4 3.3 fusion.48
  291.8 1.3 collective-permute-start.3
  293.1 4.0 collective-permute-start.2
  297.4 76.4 %all-gather.23.cloned.1.call-done = f32[3,131072]{1,0:T(4,128)} async-done(((f32[3,4096]{1,0:T(4,128)}), f32[3,131072]{1,0:T(4,128)}) %all-gather.23.cloned.1.call-update) | async-done | bytes 1572880 | tf_op jit(solution)/shard_map/all_gather | solution.py:173
  373.8 3.3 fusion.42
  378.1 85.5 %while.40 = (s32[]{:T(128)}, f32[16,1,3,2,128]{4,3,2,1,0:T(2,128)S(1)}, s32[16]{0:T(128)S(1)}, f32[1,4,40,128]{3,1,2,0:T(4,128)S(1)}, s32[32,5]{1,0:T(8,128)S(1)...) while((s32[]{:T(128)}, ...), condition=%wide.region_11.13_spmd, body=%wide.region_7.12_spmd.sunk | while | flops 4103759 | bytes 419553 | solution.py:114
  392.2 1.2 multiply_reduce_fusion.7
  435.0 1.2 multiply_reduce_fusion.7
  440.3 1.2 multiply_reduce_fusion.7
  456.4 1.2 multiply_reduce_fusion.7
  464.4 3.3 fusion.45
  467.8 78.9 %all-gather.25.cloned.1.call-done = f32[3,131072]{1,0:T(4,128)} async-done(((f32[3,4096]{1,0:T(4,128)}), f32[3,131072]{1,0:T(4,128)}) %all-gather.25.cloned.1.call-update) | async-done | bytes 1572880 | tf_op jit(solution)/shard_map/all_gather | solution.py:163
  546.7 3.3 fusion.39
  550.0 2.7 fusion.58
  553.4 81.5 %all-gather.27.cloned.1.call-done = f32[3,131072]{1,0:T(4,128)} async-done(((f32[3,4096]{1,0:T(4,128)}), f32[3,131072]{1,0:T(4,128)}) %all-gather.27.cloned.1.call-update) | async-done | bytes 1572880 | tf_op jit(solution)/shard_map/all_gather | solution.py:172
  635.0 3.3 fusion.36
  638.4 1.3 collective-permute-start.5
  639.7 4.2 collective-permute-start.4
  643.9 76.6 %all-gather.29.cloned.1.call-done = f32[3,131072]{1,0:T(4,128)} async-done(((f32[3,4096]{1,0:T(4,128)}), f32[3,131072]{1,0:T(4,128)}) %all-gather.29.cloned.1.call-update) | async-done | bytes 1572880 | tf_op jit(solution)/shard_map/all_gather | solution.py:173
  720.5 3.3 fusion.33
  724.0 81.5 %while.41 = (s32[]{:T(128)}, f32[16,1,3,2,128]{4,3,2,1,0:T(2,128)S(1)}, s32[16]{0:T(128)S(1)}, f32[1,4,40,128]{3,1,2,0:T(4,128)S(1)}, s32[32,5]{1,0:T(8,128)S(1)...) while((s32[]{:T(128)}, ...), condition=%wide.region_16.18_spmd, body=%wide.region_12.17_spmd.sunk | while | flops 4103759 | bytes 419553 | solution.py:114
  727.3 1.2 multiply_reduce_fusion.8
  732.4 1.2 multiply_reduce_fusion.8
  737.5 1.2 multiply_reduce_fusion.8
  742.6 1.2 multiply_reduce_fusion.8
  747.7 1.2 multiply_reduce_fusion.8
  752.8 1.2 multiply_reduce_fusion.8
  757.9 1.2 multiply_reduce_fusion.8
  763.0 1.2 multiply_reduce_fusion.8
  768.1 1.2 multiply_reduce_fusion.8
  773.1 1.2 multiply_reduce_fusion.8
  778.2 1.2 multiply_reduce_fusion.8
  783.3 1.2 multiply_reduce_fusion.8
  (1070 shorter events, 204.3 us)
Async XLA Ops:
  7.2 102.4 %all-gather.15.cloned.1.call-start = ((), (), s32[]{:S(2)}) async-start(), calls=%async_computation | async-start | bytes 2162688 | tf_op jit(solution)/shard_map/all_gather | solution.py:162
  8.7 191.4 %all-gather.17.cloned.1.call-start = ((), (), s32[]{:S(2)}) async-start(), calls=%async_computation.1 | async-start | bytes 2162688 | tf_op jit(solution)/shard_map/all_gather | solution.py:163
  10.4 6.7 collective-permute-start.1
  11.7 5.4 collective-permute-start
  18.0 85.6 %copy-start.3 = (f32[3,1,4096]{2,1,0:T(1,128)S(1)}, f32[3,1,4096]{2,1,0:T(1,128)}, u32[]{:S(2)}) copy-start(f32[3,1,4096]{2,1,0:T(1,128)} %param.16) | copy-start | bytes 147460
  18.0 91.5 %copy-start.2 = (f32[2,3,1,4096]{3,2,1,0:T(1,128)S(1)}, f32[2,3,1,4096]{3,2,1,0:T(1,128)}, u32[]{:S(2)}) copy-start(f32[2,3,1,4096]{3,2,1,0:T(1,128)} %param.19) | copy-start | bytes 294916
  104.4 184.1 %all-gather.19.cloned.1.call-start = ((), (), s32[]{:S(2)}) async-start(), calls=%async_computation.2 | async-start | bytes 2162688 | tf_op jit(solution)/shard_map/all_gather | solution.py:172
  206.2 167.7 %all-gather.23.cloned.1.call-start = ((), (), s32[]{:S(2)}) async-start(), calls=%async_computation.4 | async-start | bytes 2162688 | tf_op jit(solution)/shard_map/all_gather | solution.py:173
  206.7 257.7 %all-gather.21.cloned.1.call-start = ((), (), s32[]{:S(2)}) async-start(), calls=%async_computation.3 | async-start | bytes 2162688 | tf_op jit(solution)/shard_map/all_gather | solution.py:162
  291.8 5.3 copy-start
  291.8 85.3 %collective-permute-start.3 = (f32[4,1,512]{2,0,1:T(4,128)S(1)}, f32[4,1,512]{2,0,1:T(4,128)S(1)}, u32[]{:S(2)}, u32[]{:S(2)}) collective-permute-start(f32[4,1,512]{2,0,1:T(4,128)S(1)} %get-tuple-element.422), channel_id=1, source_target_pairs={{1,0},{2,1},{3,2},{4,3},{5,4},{6,5},{7,6},{8,7},{9,8},{10,9},{11,1... | collective-permute-start | bytes 24584 | tf_op jit(solution)/shard_map/ppermute | solution.py:33
  293.1 84.0 %collective-permute-start.2 = (f32[4,1,512]{2,0,1:T(4,128)S(1)}, f32[4,1,512]{2,0,1:T(4,128)S(1)}, u32[]{:S(2)}, u32[]{:S(2)}) collective-permute-start(f32[4,1,512]{2,0,1:T(4,128)S(1)} %get-tuple-element.421), channel_id=1, source_target_pairs={{0,1},{1,2},{2,3},{3,4},{4,5},{5,6},{6,7},{7,8},{8,9},{9,10},{10,1... | collective-permute-start | bytes 24584 | tf_op jit(solution)/shard_map/ppermute | solution.py:31
  297.1 249.5 %all-gather.25.cloned.1.call-start = ((), (), s32[]{:S(2)}) async-start(), calls=%async_computation.5 | async-start | bytes 2162688 | tf_op jit(solution)/shard_map/all_gather | solution.py:163
  464.4 170.6 %all-gather.27.cloned.1.call-start = ((), (), s32[]{:S(2)}) async-start(), calls=%async_computation.6 | async-start | bytes 2162688 | tf_op jit(solution)/shard_map/all_gather | solution.py:172
  552.7 167.8 %all-gather.29.cloned.1.call-start = ((), (), s32[]{:S(2)}) async-start(), calls=%async_computation.7 | async-start | bytes 2162688 | tf_op jit(solution)/shard_map/all_gather | solution.py:173
  638.4 85.6 %copy-start.1 = (f32[3,1,4096]{2,1,0:T(1,128)}, f32[3,1,4096]{2,1,0:T(1,128)S(1)}, u32[]{:S(2)}) copy-start(f32[3,1,4096]{2,1,0:T(1,128)S(1)} %transpose.74) | copy-start | bytes 147460
  638.4 85.4 %collective-permute-start.5 = (f32[4,1,512]{2,1,0:T(1,128)S(1)}, f32[4,1,512]{2,1,0:T(1,128)S(1)}, u32[]{:S(2)}, u32[]{:S(2)}) collective-permute-start(f32[4,1,512]{2,1,0:T(1,128)S(1)} %get-tuple-element.425), channel_id=1, source_target_pairs={{1,0},{2,1},{3,2},{4,3},{5,4},{6,5},{7,6},{8,7},{9,8},{10,9},{11,1... | collective-permute-start | bytes 24584 | tf_op jit(solution)/shard_map/ppermute | solution.py:33
  639.7 84.1 %collective-permute-start.4 = (f32[4,1,512]{2,1,0:T(1,128)S(1)}, f32[4,1,512]{2,1,0:T(1,128)S(1)}, u32[]{:S(2)}, u32[]{:S(2)}) collective-permute-start(f32[4,1,512]{2,1,0:T(1,128)S(1)} %get-tuple-element.424), channel_id=1, source_target_pairs={{0,1},{1,2},{2,3},{3,4},{4,5},{5,6},{6,7},{7,8},{8,9},{9,10},{10,1... | collective-permute-start | bytes 24584 | tf_op jit(solution)/shard_map/ppermute | solution.py:31
Sparse Core Ops, SparseCore 0:
  11.3 91.7 all-gather.14
  106.5 93.5 all-gather.16
  206.3 82.1 all-gather.18
  291.7 82.1 all-gather.22
  377.0 82.2 all-gather.20
  464.5 82.1 all-gather.24
  552.8 82.1 all-gather.26
  638.3 82.1 all-gather.28
where the time goes:
time: 815 us; the launch traced here: 813 us
  waiting for transfers between devices  484 us (59%)
  local copies, waits for them, and re-layouts  128 us (16%)
  other arithmetic  107 us (13%)
  loops' own time  36.5 us (4%)
  matrix products  26.4 us (3%)
  starting transfers between devices  17.1 us (2%)
  between operations  14.6 us (2%)
    all_gather x2, waiting for transfers between devices, body(): lax.all_gather(moment, 'bead', axis=1, tiled=True)  166 us
    all_gather x2, waiting for transfers between devices, body(): lax.all_gather(next_coords, 'bead', axis=1, tiled=True)  163 us
    all_gather x2, waiting for transfers between devices, body(): lax.all_gather(next_moment, 'bead', axis=1, tiled=True)  153 us
    reduce_sum x48, other arithmetic, tile_force(): force_x = own_rows[3] * jnp.sum(weight * delta_x, axis=(1, 3))  55.4 us
    another operation x3, loops' own time, bead_forces(): lax.map(group_force, jnp.arange(block_count // group_size, dtype=jnp.int32))  36.5 us
    sub x144, local copies, waits for them, and re-layouts, tile_force(): delta_y = own_rows[1][:, None, :, None] - tile_rows[1][:, :, None, :]  30.8 us
    mul x48, other arithmetic, tile_force(): force_x = own_rows[3] * jnp.sum(weight * delta_x, axis=(1, 3))  30.4 us
    dynamic_slice x48, local copies, waits for them, and re-layouts, bead_forces(): lax.map(group_force, jnp.arange(block_count // group_size, dtype=jnp.int32))  28 us
  transfers between devices with their start and end apart: 14, of which 6 were waited for; matrix products, arithmetic and copies ran while one was open for 22% of the time, Pallas kernels for 0%

commit v1 on v0

v1 whole, which is shorter than its diff:
```python
import functools
import math

import jax
import jax.numpy as jnp
import numpy as np
from jax import lax
from jax.experimental import pallas as pl
from jax.experimental.pallas import tpu as pltpu
from jax.sharding import PartitionSpec as P

MESH = pl.DeviceIdType.MESH
F32 = jnp.float32
BF16 = jnp.bfloat16
LANES = 128
HALO = 4
NBR = 5
ROWS = 48
half_step = 0.025
time_step = 0.05
chain_freq = 12.0
thermal = 0.375
screening = 4.0
softening = 0.09
decay = math.log2(math.e) / screening
highest = lax.Precision.HIGHEST


def mode_matrix(n):
    j = np.arange(n)[:, None]
    k = np.arange(n)[None, :]
    phase = 2.0 * np.pi * j * k / n
    plain, paired = 1.0 / math.sqrt(n), math.sqrt(2.0 / n)
    return np.where(
        k == 0,
        plain,
        np.where(
            k < n // 2,
            paired * np.cos(phase),
            np.where(k == n // 2, plain * np.cos(phase), paired * np.sin(phase)),
        ),
    ).astype(np.float32)


def mode_tables(n):
    k = np.arange(n)
    w = 2.0 * chain_freq * np.sin(np.pi * k / n)
    angle = w * time_step
    ratio = np.where(k == 0, time_step, np.sin(angle) / np.where(k == 0, 1.0, w))
    friction = np.where(k == 0, 1.0, 2.0 * w)
    damping = np.exp(-friction * time_step)
    kick = np.sqrt(1.0 - damping * damping)
    tables = np.stack([np.cos(angle), ratio, w * np.sin(angle), damping, kick])
    return np.repeat(tables[:, :, None], LANES, axis=2).astype(np.float32)


def shift_table():
    parts = {0: (0, 0), 1: (1, 0), 2: (2, 0), 3: (2, 1), 4: (4, 0)}
    table = np.ones((2 * HALO + 1, ROWS), np.float32)
    for s in range(-HALO, HALO + 1):
        sign = -1 if s < 0 else 1
        one, two = parts[abs(s)]
        table[s + HALO, 27] = s * s
        table[s + HALO, 28:32] = -2 * s
        table[s + HALO, 32:36] = sign * one
        table[s + HALO, 36:40] = sign * two
    return np.repeat(table[:, :, None], LANES, axis=2)


def charge_of(types):
    return jnp.where(
        types == 0, 1.0, jnp.where(types == 1, -1.0, jnp.where(types == 2, 0.6, -1.4))
    ).astype(F32)


def three(v):
    high = v.astype(BF16).astype(F32)
    rest = v - high
    mid = rest.astype(BF16).astype(F32)
    return high, mid, rest - mid


def kernel(
    nb,
    ns,
    lists,
    x_ref,
    p_ref,
    noise_ref,
    types_ref,
    mult_ref,
    to_mode,
    to_bead,
    tab_ref,
    x_out,
    p_out,
    xin,
    pin,
    nin,
    ext,
    extq,
    fout,
    fin,
    xs,
    ps,
    pbuf,
    modes,
    fe,
    fb,
    fa,
    s_in,
    r_in,
    s_h,
    r_h,
    s_f,
    r_f,
    s_x,
    r_x,
    s_xh,
    r_xh,
    s_p,
    r_p,
):
    me = lax.axis_index("bead")
    dom = lax.axis_index("space")
    first = dom * nb
    lower, upper = dom > 0, dom < ns - 1

    def lanes(block):
        return pl.ds(pl.multiple_of(block * LANES, LANES), LANES)

    def remote(src, dst, send, recv, bead, space):
        return pltpu.make_async_remote_copy(
            src_ref=src,
            dst_ref=dst,
            send_sem=send,
            recv_sem=recv,
            device_id=(bead, space),
            device_id_type=MESH,
        )

    def arrived(ref, sem):
        pltpu.make_async_copy(ref, ref, sem).wait()

    def others(body):
        def step(i, carry):
            body(lax.rem(me + i, nb))
            return carry

        lax.fori_loop(1, nb, step, 0)

    def loop(begin, end, body):
        def step(i, carry):
            body(i)
            return carry

        lax.fori_loop(begin, end, step, 0)

    barrier = pltpu.get_barrier_semaphore()

    def greet(bead, space):
        pl.semaphore_signal(barrier, inc=1, device_id=(bead, space), device_id_type=MESH)

    others(lambda t: greet(t, dom))

    @pl.when(lower)
    def _():
        loop(nb - HALO, nb, lambda t: greet(t, dom - 1))

        @pl.when(me < nb - HALO)
        def _():
            greet(me, dom - 1)

    @pl.when(upper)
    def _():
        loop(0, HALO, lambda t: greet(t, dom + 1))

        @pl.when(me >= HALO)
        def _():
            greet(me, dom + 1)

    row8 = lax.broadcasted_iota(jnp.int32, (4, LANES), 0)
    last = row8 == 3
    ones4 = jnp.ones((4, LANES), F32)
    zero4 = jnp.zeros((4, LANES), F32)
    minus4 = jnp.where(last, 0.0, -1.0)

    def centred(turn, n):
        return [ext[turn, n, c] - 1.0 for c in range(3)]

    def features(turn, n, own):
        x, y, z = centred(turn, n)
        q = extq[n]
        norm = x * x + y * y + z * z
        v = jnp.concatenate(
            [x, y, z, norm, norm + softening, norm, norm, norm], axis=0
        )
        high, mid, low = three(v)
        h4, m4, l4 = high[0:4], mid[0:4], low[0:4]
        hx, mx, lx = high[0:1], mid[0:1], low[0:1]
        split_x = jnp.concatenate([hx, mx, lx, jnp.zeros_like(hx)], axis=0)
        left = jnp.concatenate(
            [h4, m4, l4, h4, m4, h4, ones4, split_x, minus4, minus4, zero4, zero4],
            axis=0,
        )
        fe[n] = left.T.astype(BF16)
        heavy = jnp.concatenate([x, y, z, jnp.ones_like(x)], axis=0) * q
        qh, qm, ql = three(heavy)
        fb[n] = jnp.concatenate([qh, qm, ql, zero4], axis=0).astype(BF16)
        if own:
            ah = jnp.where(last, 1.0, -2.0 * h4)
            am = jnp.where(last, 0.0, -2.0 * m4)
            al = jnp.where(last, 0.0, -2.0 * l4)
            square = jnp.concatenate(
                [high[4:5], mid[4:5], low[4:5], jnp.ones_like(x)], axis=0
            )
            unit = jnp.where(last, 0.0, 1.0)
            twice = -2.0 * split_x
            right = jnp.concatenate(
                [ah, ah, ah, am, am, al, square, unit, twice, twice, zero4, zero4],
                axis=0,
            )
            fa[n - HALO] = right.astype(BF16)

    def force(turn, b):
        base = fa[b]
        total = jnp.zeros((16, LANES), F32)
        moved = jnp.zeros((16, LANES), F32)
        for m in range(NBR):
            listed = lists[b, m]
            n = jnp.clip(listed - first + HALO, 0, nb + 2 * HALO - 1)
            s = jnp.clip(first + b - listed, -HALO, HALO)
            right = base * mult_ref[s + HALO]
            square = jnp.dot(fe[n], right, preferred_element_type=F32)
            r = lax.rsqrt(square)
            weight = jnp.exp2((square * r) * (-decay)) * ((r * r) * (r + 0.25))
            high = weight.astype(BF16)
            low = (weight - high.astype(F32)).astype(BF16)
            left = fb[n]
            part = jnp.dot(
                jnp.concatenate([left, left], axis=1),
                jnp.concatenate([high, low], axis=0),
                preferred_element_type=F32,
            )
            total = total + part
            moved = moved + s.astype(F32) * part
        sums = total[0:4] + total[4:8] + total[8:12]
        shifted = moved[3:4] + moved[7:8] + moved[11:12]
        x, y, z = centred(turn, b + HALO)
        q = extq[b + HALO]
        plain = sums[3:4]
        fx = q * (x * plain + shifted - sums[0:1])
        fy = q * (y * plain - sums[1:2])
        fz = q * (z * plain - sums[2:3])
        return fx, fy, fz

    def send_force(turn, b):
        fx, fy, fz = force(turn, b)
        fout[turn, b, 0] = fx
        fout[turn, b, 1] = fy
        fout[turn, b, 2] = fz

        @pl.when(b != me)
        def _():
            remote(fout.at[turn, b], fin.at[turn, me], s_f.at[turn], r_f.at[turn], b, dom).start()

    def gather_force(turn):
        fin[turn, me] = fout[turn, me]
        arrived(fin.at[turn, pl.ds(0, nb - 1)], r_f.at[turn])

    def load_own(b):
        ext[0, HALO + b] = x_ref[:, :, lanes(b)]
        extq[HALO + b] = charge_of(types_ref[pl.ds(b, 1), :])

    loop(0, nb, load_own)

    @pl.when(jnp.logical_not(lower))
    def _():
        for t in range(3):
            ext[t, 0:HALO] = jnp.zeros((HALO, 3, 1, LANES), F32)
        extq[0:HALO] = jnp.zeros((HALO, 1, LANES), F32)

    @pl.when(jnp.logical_not(upper))
    def _():
        for t in range(3):
            ext[t, nb + HALO : nb + 2 * HALO] = jnp.zeros((HALO, 3, 1, LANES), F32)
        extq[nb + HALO : nb + 2 * HALO] = jnp.zeros((HALO, 1, LANES), F32)

    loop(HALO, nb + HALO, lambda n: features(0, n, True))

    senders = (
        nb
        - 1
        + jnp.where(lower, jnp.where(me < HALO, nb, 1), 0)
        + jnp.where(upper, jnp.where(me >= nb - HALO, nb, 1), 0)
    )
    pl.semaphore_wait(barrier, senders)

    low_edge, low_halo = pl.ds(HALO, HALO), pl.ds(0, HALO)
    high_edge, high_halo = pl.ds(nb, HALO), pl.ds(nb + HALO, HALO)

    def down():
        return [
            remote(ext.at[0, low_edge], ext.at[0, high_halo], s_h.at[0], r_h.at[0], me, dom - 1),
            remote(extq.at[low_edge], extq.at[high_halo], s_h.at[1], r_h.at[1], me, dom - 1),
        ]

    def up():
        return [
            remote(ext.at[0, high_edge], ext.at[0, low_halo], s_h.at[2], r_h.at[2], me, dom + 1),
            remote(extq.at[high_edge], extq.at[low_halo], s_h.at[3], r_h.at[3], me, dom + 1),
        ]

    @pl.when(lower)
    def _():
        for copy in down():
            copy.start()

    @pl.when(upper)
    def _():
        for copy in up():
            copy.start()

    def send_start(t):
        remote(x_ref.at[:, :, lanes(t)], xin.at[me], s_in.at[0], r_in.at[0], t, dom).start()
        remote(p_ref.at[:, :, lanes(t)], pin.at[me], s_in.at[1], r_in.at[1], t, dom).start()
        remote(noise_ref.at[0, :, :, lanes(t)], nin.at[0, me], s_in.at[2], r_in.at[2], t, dom).start()

    def send_noise(t):
        remote(noise_ref.at[1, :, :, lanes(t)], nin.at[1, me], s_in.at[3], r_in.at[3], t, dom).start()

    others(send_start)
    xin[me] = x_ref[:, :, lanes(me)]
    pin[me] = p_ref[:, :, lanes(me)]
    nin[0, me] = noise_ref[0, :, :, lanes(me)]
    nin[1, me] = noise_ref[1, :, :, lanes(me)]

    inner = nb - 2 * HALO
    if inner > 0:
        loop(0, inner, lambda i: send_force(0, HALO + lax.rem(me + i, inner)))

    @pl.when(upper)
    def _():
        arrived(ext.at[0, high_halo], r_h.at[0])
        arrived(extq.at[high_halo], r_h.at[1])

    @pl.when(lower)
    def _():
        arrived(ext.at[0, low_halo], r_h.at[2])
        arrived(extq.at[low_halo], r_h.at[3])

    loop(0, HALO, lambda n: features(0, n, False))
    loop(nb + HALO, nb + 2 * HALO, lambda n: features(0, n, False))

    def edge(i):
        spot = lax.rem(me + i, 2 * HALO)
        send_force(0, jnp.where(spot < HALO, spot, spot + inner))

    loop(0, 2 * HALO, edge)
    others(send_noise)

    mass = (types_ref[pl.ds(me, 1), :] + 1).astype(F32)
    width = jnp.sqrt(thermal * mass)
    inverse = 1.0 / mass
    cosine, ratio, stiffness, damping, kick = [tab_ref[i] for i in range(5)]

    def component(ref, lead, c):
        return jnp.concatenate([ref[(*lead, j, c)] for j in range(nb)], axis=0)

    def times(matrix, parts):
        whole = jnp.concatenate(parts, axis=1)
        out = jnp.dot(matrix[...], whole, precision=highest, preferred_element_type=F32)
        return [out[:, LANES * i : LANES * (i + 1)] for i in range(len(parts))]

    def drift(turn, mode_x, mode_p):
        next_x, next_p = [], []
        for c in range(3):
            noise = component(nin, (turn,), c)
            p_new = damping * mode_p[c] + kick * width * noise
            next_x.append(cosine * mode_x[c] + ratio * p_new * inverse)
            next_p.append(cosine * p_new - stiffness * mass * mode_x[c])
        return next_x, next_p

    def spread(ref, lead, parts):
        for c in range(3):
            for j in range(nb):
                ref[(*lead, j, c)] = parts[c][j : j + 1]

    def send_coords(turn):
        others(
            lambda t: remote(
                xs.at[turn - 1, t],
                ext.at[turn, HALO + me],
                s_x.at[turn - 1],
                r_x.at[turn - 1],
                t,
                dom,
            ).start()
        )

        @pl.when(jnp.logical_and(lower, me < HALO))
        def _():
            loop(
                0,
                nb,
                lambda t: remote(
                    xs.at[turn - 1, lax.rem(me + t, nb)],
                    ext.at[turn, nb + HALO + me],
                    s_xh.at[turn - 1],
                    r_xh.at[turn - 1, 0],
                    lax.rem(me + t, nb),
                    dom - 1,
                ).start(),
            )

        @pl.when(jnp.logical_and(upper, me >= nb - HALO))
        def _():
            loop(
                0,
                nb,
                lambda t: remote(
                    xs.at[turn - 1, lax.rem(me + t, nb)],
                    ext.at[turn, me - (nb - HALO)],
                    s_xh.at[turn - 1],
                    r_xh.at[turn - 1, 1],
                    lax.rem(me + t, nb),
                    dom + 1,
                ).start(),
            )

        ext[turn, HALO + me] = xs[turn - 1, me]

    def gather_coords(turn):
        arrived(ext.at[turn, pl.ds(0, nb - 1)], r_x.at[turn - 1])

        @pl.when(upper)
        def _():
            arrived(ext.at[turn, pl.ds(0, HALO)], r_xh.at[turn - 1, 0])

        @pl.when(lower)
        def _():
            arrived(ext.at[turn, pl.ds(0, HALO)], r_xh.at[turn - 1, 1])

    def all_features(turn):
        loop(HALO, nb + HALO, lambda n: features(turn, n, True))
        loop(0, HALO, lambda n: features(turn, n, False))
        loop(nb + HALO, nb + 2 * HALO, lambda n: features(turn, n, False))

    some = pl.ds(0, nb - 1)
    arrived(xin.at[some], r_in.at[0])
    arrived(pin.at[some], r_in.at[1])
    arrived(nin.at[0, some], r_in.at[2])
    gather_force(0)
    parts = [component(xin, (), c) for c in range(3)] + [
        component(pin, (), c) + half_step * component(fin, (0,), c) for c in range(3)
    ]
    parts = times(to_mode, parts)
    mode_x, mode_p = drift(0, parts[:3], parts[3:])
    spread(xs, (0,), times(to_bead, mode_x))
    send_coords(1)
    for c in range(3):
        modes[c] = mode_x[c]
        modes[3 + c] = mode_p[c]

    gather_coords(1)
    all_features(1)
    loop(0, nb, lambda i: send_force(1, lax.rem(me + i, nb)))
    arrived(nin.at[1, some], r_in.at[3])
    gather_force(1)
    kicks = times(to_mode, [component(fin, (1,), c) for c in range(3)])
    mode_x, mode_p = drift(
        1,
        [modes[c] for c in range(3)],
        [modes[3 + c] + 2.0 * half_step * kicks[c] for c in range(3)],
    )
    spread(xs, (1,), times(to_bead, mode_x))
    send_coords(2)
    spread(ps, (), times(to_bead, mode_p))
    others(lambda t: remote(ps.at[t], pbuf.at[me], s_p, r_p, t, dom).start())
    pbuf[me] = ps[me]

    gather_coords(2)
    all_features(2)
    arrived(pbuf.at[some], r_p)

    def finish(b):
        for c, f in enumerate(force(2, b)):
            x_out[c, :, lanes(b)] = ext[2, HALO + b, c]
            p_out[c, :, lanes(b)] = pbuf[b, c] + half_step * f

    loop(0, nb, finish)

    arrived(xin.at[some], s_in.at[0])
    arrived(pin.at[some], s_in.at[1])
    arrived(nin.at[0, some], s_in.at[2])
    arrived(nin.at[1, some], s_in.at[3])
    for turn in range(2):
        arrived(fin.at[turn, some], s_f.at[turn])
        arrived(xs.at[turn, some], s_x.at[turn])

        @pl.when(jnp.logical_or(jnp.logical_and(lower, me < HALO), jnp.logical_and(upper, me >= nb - HALO)))
        def _():
            arrived(xs.at[turn], s_xh.at[turn])

    arrived(ps.at[some], s_p)

    @pl.when(lower)
    def _():
        for copy in down():
            copy.wait_send()

    @pl.when(upper)
    def _():
        for copy in up():
            copy.wait_send()


def solution(mesh):
    nb, ns = mesh.shape["bead"], mesh.shape["space"]

    def body(positions, momenta, atom_types, neighbours, thermal_noise):
        matrix = mode_matrix(nb)
        vmem = pl.BlockSpec(memory_space=pltpu.VMEM)
        piece = (3, 1, LANES)
        dma = pltpu.SemaphoreType.DMA
        return pl.pallas_call(
            functools.partial(kernel, nb, ns),
            out_shape=(
                jax.ShapeDtypeStruct(positions.shape, F32),
                jax.ShapeDtypeStruct(momenta.shape, F32),
            ),
            in_specs=[pl.BlockSpec(memory_space=pltpu.SMEM)] + [vmem] * 8,
            out_specs=(vmem, vmem),
            scratch_shapes=[
                pltpu.VMEM((nb, *piece), F32),
                pltpu.VMEM((nb, *piece), F32),
                pltpu.VMEM((2, nb, *piece), F32),
                pltpu.VMEM((3, nb + 2 * HALO, *piece), F32),
                pltpu.VMEM((nb + 2 * HALO, 1, LANES), F32),
                pltpu.VMEM((2, nb, *piece), F32),
                pltpu.VMEM((2, nb, *piece), F32),
                pltpu.VMEM((2, nb, *piece), F32),
                pltpu.VMEM((nb, *piece), F32),
                pltpu.VMEM((nb, *piece), F32),
                pltpu.VMEM((6, nb, LANES), F32),
                pltpu.VMEM((nb + 2 * HALO, LANES, ROWS), BF16),
                pltpu.VMEM((nb + 2 * HALO, 16, LANES), BF16),
                pltpu.VMEM((nb, ROWS, LANES), BF16),
                dma((4,)),
                dma((4,)),
                dma((4,)),
                dma((4,)),
                dma((2,)),
                dma((2,)),
                dma((2,)),
                dma((2,)),
                dma((2,)),
                dma((2, 2)),
                dma,
                dma,
            ],
            compiler_params=pltpu.CompilerParams(
                collective_id=0, has_side_effects=True, vmem_limit_bytes=32 * 1024 * 1024
            ),
            name="path_integral_steps",
        )(
            neighbours,
            positions,
            momenta,
            thermal_noise,
            atom_types.reshape(nb, LANES),
            jnp.asarray(shift_table(), BF16),
            jnp.asarray(matrix.T.copy()),
            jnp.asarray(matrix),
            jnp.asarray(mode_tables(nb)),
        )

    spec = P(None, "bead", "space")
    return jax.shard_map(
        body,
        mesh=mesh,
        in_specs=(spec, spec, P("space"), P("space", None), P(None, None, "bead", "space")),
        out_specs=(spec, spec),
        check_vma=False,
    )
```

time: 815 us -> 94.7 us (0.12)
  waiting for transfers between devices: 484 us -> 0 us
  local copies, waits for them, and re-layouts: 128 us -> 7.72 us
  other arithmetic: 107 us -> 0 us
  Pallas kernels: 0 us -> 84.9 us
  loops' own time: 36.5 us -> 0 us
  matrix products: 26.4 us -> 0 us
  starting transfers between devices: 17.1 us -> 0 us
  between operations: 14.6 us -> 0.65 us
    all_gather x8 -> x0, waiting for transfers between devices: 482 us -> none  [the longest x2 166 us: body(): lax.all_gather(moment, 'bead', axis=1, tiled=True)]
    pallas_call x0 -> x1, Pallas kernels: none -> 84.9 us  [body(): pl.pallas_call(functools.partial(kernel, nb, ns), out_shape=(jax.ShapeDty...]
    reduce_sum x49 -> x0, other arithmetic: 56.3 us -> none  [the longest x48 55.4 us: tile_force(): force_x = own_rows[3] * jnp.sum(weight * delta_x, axis=(1, 3))]
    another operation x3 -> x0, loops' own time: 36.5 us -> none  [bead_forces(): lax.map(group_force, jnp.arange(block_count // group_size, dtype=jnp.int32))]
    mul x54 -> x0, other arithmetic: 31.9 us -> none  [the longest x48 30.4 us: tile_force(): force_x = own_rows[3] * jnp.sum(weight * delta_x, axis=(1, 3))]
    dynamic_slice x102 -> x0, local copies, waits for them, and re-layouts: 31.7 us -> none  [the longest x48 28 us: bead_forces(): lax.map(group_force, jnp.arange(block_count // group_size, dtype=jnp.int32))]
    sub x240 -> x0, local copies, waits for them, and re-layouts: 31.1 us -> none  [the longest x144 30.8 us: tile_force(): delta_y = own_rows[1][:, None, :, None] - tile_rows[1][:, :, None, :]]
    while x50 -> x0, local copies, waits for them, and re-layouts: 28 us -> none  [the longest x48 28 us: group_force(): lax.dynamic_slice_in_dim(extended, first_block + begin_row, group_size, 1)]
  transfers between devices with their start and end apart: 14 -> 0, of which waited for: 6 -> 0; matrix products, arithmetic and copies ran while one was open for 22% -> 0% of each run, Pallas kernels for 0% -> 0%
where the time goes in v1:
time: 94.7 us; the launch traced here: 93.3 us
  Pallas kernels  84.9 us (90%)
  local copies, waits for them, and re-layouts  7.72 us (8%)
    pallas_call x1, Pallas kernels, body(): pl.pallas_call(functools.partial(kernel, nb, ns), out_shape=(jax.ShapeDty...  84.9 us
    unnamed x19, local copies, waits for them, and re-layouts  7.72 us

profile of v1, /device:TPU:1, one launch (start us, length us, event | category | flops | bytes accessed | tf_op | source)
XLA Modules:
  0.0 93.3 jit_solution(2659653195347284704)
XLA Ops:
  0.6 0.0 copy-start.5
  0.6 0.8 copy.11.lists
  1.4 0.0 copy-done.5
  1.4 0.0 copy-start
  1.4 0.9 copy-done
  2.3 0.0 copy-start.1
  2.3 0.9 copy-done.1
  3.2 0.0 copy-start.2
  3.2 0.9 copy-done.2
  4.1 0.0 copy-start.3
  4.1 0.8 copy-done.3
  4.9 0.0 copy-start.4
  4.9 0.8 copy-done.4
  5.7 0.0 copy-start.6
  5.7 0.7 copy-done.6
  6.4 0.0 copy-start.7
  6.4 0.7 copy-done.7
  7.1 84.9 %path_integral_steps.1 = (f32[3,1,4096]{2,1,0:T(1,128)S(1)}, f32[3,1,4096]{2,1,0:T(1,128)S(1)}) custom-call(s32[32,5]{1,0:T(8,128)S(1)} %copy.11.lists, f32[3,1,4096]{2,1,0:T(1,128)S(1)} %copy-done.3, f32[3,1,4096]{2,1,0:T(1,128)S(1)} %copy-done.4, f32[2,3,1,4096]{3,2,1,0:T(1,128)S(1)} %copy-done.1, s32[32,128]{1,0:T(8,128)S(1)} %bitcast.1, ...), custom_call_target="tpu_custom_call" | custom-call | tf_op jit(solution)/shard_map/path_integral_steps/pallas_call | solution.py:526
  92.1 0.6 copy.14
  92.7 0.6 copy.15
Async XLA Ops:
  0.6 0.8 copy-start.5
  1.4 0.9 copy-start
  2.3 0.9 copy-start.1
  3.2 0.9 copy-start.2
  4.1 0.8 copy-start.3
  4.9 0.8 copy-start.4
  5.7 0.7 copy-start.6
  6.4 0.7 copy-start.7

commit v2 on v1

--- a/solution.py
+++ b/solution.py
@@ -84,16 +84,22 @@
     nb,
     ns,
     lists,
+    x_hbm,
+    p_hbm,
+    noise_hbm,
+    types_hbm,
+    mult_hbm,
+    to_mode_hbm,
+    to_bead_hbm,
+    tab_hbm,
+    x_out,
+    p_out,
     x_ref,
-    p_ref,
-    noise_ref,
     types_ref,
     mult_ref,
     to_mode,
     to_bead,
     tab_ref,
-    x_out,
-    p_out,
     xin,
     pin,
     nin,
@@ -120,6 +126,9 @@
     r_xh,
     s_p,
     r_p,
+    s_own,
+    even,
+    odd,
 ):
     me = lax.axis_index("bead")
     dom = lax.axis_index("space")
@@ -156,6 +165,25 @@
 
         lax.fori_loop(begin, end, step, 0)
 
+    staged = [
+        pltpu.make_async_copy(src, dst, s_own.at[i])
+        for i, (src, dst) in enumerate(
+            [
+                (x_hbm, x_ref),
+                (types_hbm, types_ref),
+                (mult_hbm, mult_ref),
+                (to_mode_hbm, to_mode),
+                (to_bead_hbm, to_bead),
+                (tab_hbm, tab_ref),
+                (p_hbm.at[:, :, lanes(me)], pin.at[me]),
+                (noise_hbm.at[0, :, :, lanes(me)], nin.at[0, me]),
+                (noise_hbm.at[1, :, :, lanes(me)], nin.at[1, me]),
+            ]
+        )
+    ]
+    for copy in staged:
+        copy.start()
+
     barrier = pltpu.get_barrier_semaphore()
 
     def greet(bead, space):
@@ -188,7 +216,22 @@
     def centred(turn, n):
         return [ext[turn, n, c] - 1.0 for c in range(3)]
 
-    def features(turn, n, own):
+    def features(turn, begin, count, own):
+        group = 4
+
+        def several(i):
+            done = [one_features(turn, begin + group * i + k, own) for k in range(group)]
+            for k, (left, heavy, right) in enumerate(done):
+                n = begin + group * i + k
+                fe[n] = left
+                fb[n] = heavy
+                if own:
+                    fa[n - HALO] = right
+
+        loop(0, count // group, several)
+
+    def one_features(turn, n, own):
+        right = None
         x, y, z = centred(turn, n)
         q = extq[n]
         norm = x * x + y * y + z * z
@@ -203,10 +246,9 @@
             [h4, m4, l4, h4, m4, h4, ones4, split_x, minus4, minus4, zero4, zero4],
             axis=0,
         )
-        fe[n] = left.T.astype(BF16)
         heavy = jnp.concatenate([x, y, z, jnp.ones_like(x)], axis=0) * q
         qh, qm, ql = three(heavy)
-        fb[n] = jnp.concatenate([qh, qm, ql, zero4], axis=0).astype(BF16)
+        heavy = jnp.concatenate([qh, qm, ql, zero4], axis=0).astype(BF16)
         if own:
             ah = jnp.where(last, 1.0, -2.0 * h4)
             am = jnp.where(last, 0.0, -2.0 * m4)
@@ -220,18 +262,26 @@
                 [ah, ah, ah, am, am, al, square, unit, twice, twice, zero4, zero4],
                 axis=0,
             )
-            fa[n - HALO] = right.astype(BF16)
-
-    def force(turn, b):
+            right = right.astype(BF16)
+        return left.T.astype(BF16), heavy, right
+
+    def squares(b, ref):
         base = fa[b]
+        for m in range(NBR):
+            listed = lists[m, b]
+            n = jnp.clip(listed - first + HALO, 0, nb + 2 * HALO - 1)
+            s = jnp.clip(first + b - listed, -HALO, HALO)
+            right = base * mult_ref[s + HALO]
+            ref[m] = jnp.dot(fe[n], right, preferred_element_type=F32)
+
+    def force(turn, b, ref):
         total = jnp.zeros((16, LANES), F32)
         moved = jnp.zeros((16, LANES), F32)
         for m in range(NBR):
-            listed = lists[b, m]
+            listed = lists[m, b]
             n = jnp.clip(listed - first + HALO, 0, nb + 2 * HALO - 1)
             s = jnp.clip(first + b - listed, -HALO, HALO)
-            right = base * mult_ref[s + HALO]
-            square = jnp.dot(fe[n], right, preferred_element_type=F32)
+            square = ref[m]
             r = lax.rsqrt(square)
             weight = jnp.exp2((square * r) * (-decay)) * ((r * r) * (r + 0.25))
             high = weight.astype(BF16)
@@ -254,16 +304,44 @@
         fz = q * (z * plain - sums[2:3])
         return fx, fy, fz
 
+    def forces(turn, count, block_of, take, beside=None):
+        squares(block_of(0), even)
+        group = 4 if count % 4 == 0 else 2
+
+        def several(i):
+            blocks = [block_of(lax.rem(group * i + k, count)) for k in range(group + 1)]
+            done = []
+            for k in range(group):
+                here, there = (odd, even) if k % 2 else (even, odd)
+                squares(blocks[k + 1], there)
+                done.append((blocks[k], force(turn, blocks[k], here)))
+            take(done)
+            if beside is not None:
+                beside(i)
+
+        loop(0, count // group, several)
+
+    def keep_force(turn):
+        def take(done):
+            for b, parts in done:
+                for c in range(3):
+                    fout[turn, b, c] = parts[c]
+
+        return take
+
     def send_force(turn, b):
-        fx, fy, fz = force(turn, b)
-        fout[turn, b, 0] = fx
-        fout[turn, b, 1] = fy
-        fout[turn, b, 2] = fz
-
         @pl.when(b != me)
         def _():
             remote(fout.at[turn, b], fin.at[turn, me], s_f.at[turn], r_f.at[turn], b, dom).start()
 
+    def send_forces(turn):
+        def take(done):
+            keep_force(turn)(done)
+            for b, _ in done:
+                send_force(turn, b)
+
+        return take
+
     def gather_force(turn):
         fin[turn, me] = fout[turn, me]
         arrived(fin.at[turn, pl.ds(0, nb - 1)], r_f.at[turn])
@@ -272,6 +350,8 @@
         ext[0, HALO + b] = x_ref[:, :, lanes(b)]
         extq[HALO + b] = charge_of(types_ref[pl.ds(b, 1), :])
 
+    staged[0].wait()
+    staged[1].wait()
     loop(0, nb, load_own)
 
     @pl.when(jnp.logical_not(lower))
@@ -286,7 +366,17 @@
             ext[t, nb + HALO : nb + 2 * HALO] = jnp.zeros((HALO, 3, 1, LANES), F32)
         extq[nb + HALO : nb + 2 * HALO] = jnp.zeros((HALO, 1, LANES), F32)
 
-    loop(HALO, nb + HALO, lambda n: features(0, n, True))
+    features(0, HALO, nb, True)
+    staged[2].wait()
+    inner = nb - 2 * HALO
+    early = inner // 6 * 2
+    late = inner - early
+
+    def inner_block(i):
+        return HALO + lax.rem(me + i, inner)
+
+    if early > 0:
+        forces(0, early, inner_block, keep_force(0))
 
     senders = (
         nb
@@ -322,22 +412,30 @@
             copy.start()
 
     def send_start(t):
-        remote(x_ref.at[:, :, lanes(t)], xin.at[me], s_in.at[0], r_in.at[0], t, dom).start()
-        remote(p_ref.at[:, :, lanes(t)], pin.at[me], s_in.at[1], r_in.at[1], t, dom).start()
-        remote(noise_ref.at[0, :, :, lanes(t)], nin.at[0, me], s_in.at[2], r_in.at[2], t, dom).start()
+        remote(x_hbm.at[:, :, lanes(t)], xin.at[me], s_in.at[0], r_in.at[0], t, dom).start()
+        remote(p_hbm.at[:, :, lanes(t)], pin.at[me], s_in.at[1], r_in.at[1], t, dom).start()
+        remote(noise_hbm.at[0, :, :, lanes(t)], nin.at[0, me], s_in.at[2], r_in.at[2], t, dom).start()
 
     def send_noise(t):
-        remote(noise_ref.at[1, :, :, lanes(t)], nin.at[1, me], s_in.at[3], r_in.at[3], t, dom).start()
-
-    others(send_start)
+        remote(noise_hbm.at[1, :, :, lanes(t)], nin.at[1, me], s_in.at[3], r_in.at[3], t, dom).start()
+
+    rounds = max(late // (4 if late % 4 == 0 else 2), 1)
+    beside = (nb - 1) // rounds if late > 0 else 0
+
+    def send_started(begin, end):
+        loop(begin, end, lambda i: send_start(lax.rem(me + i, nb)))
+
     xin[me] = x_ref[:, :, lanes(me)]
-    pin[me] = p_ref[:, :, lanes(me)]
-    nin[0, me] = noise_ref[0, :, :, lanes(me)]
-    nin[1, me] = noise_ref[1, :, :, lanes(me)]
-
-    inner = nb - 2 * HALO
-    if inner > 0:
-        loop(0, inner, lambda i: send_force(0, HALO + lax.rem(me + i, inner)))
+    send_started(1 + beside * rounds, nb)
+    if early > 0:
+        loop(0, early, lambda i: send_force(0, inner_block(i)))
+    if late > 0:
+
+        def send_beside(i):
+            for k in range(beside):
+                send_start(lax.rem(me + 1 + beside * i + k, nb))
+
+        forces(0, late, lambda i: inner_block(early + i), send_forces(0), send_beside)
 
     @pl.when(upper)
     def _():
@@ -349,16 +447,18 @@
         arrived(ext.at[0, low_halo], r_h.at[2])
         arrived(extq.at[low_halo], r_h.at[3])
 
-    loop(0, HALO, lambda n: features(0, n, False))
-    loop(nb + HALO, nb + 2 * HALO, lambda n: features(0, n, False))
+    features(0, 0, HALO, False)
+    features(0, nb + HALO, HALO, False)
 
     def edge(i):
         spot = lax.rem(me + i, 2 * HALO)
-        send_force(0, jnp.where(spot < HALO, spot, spot + inner))
-
-    loop(0, 2 * HALO, edge)
+        return jnp.where(spot < HALO, spot, spot + inner)
+
+    forces(0, 2 * HALO, edge, send_forces(0))
     others(send_noise)
 
+    for copy in staged[3:]:
+        copy.wait()
     mass = (types_ref[pl.ds(me, 1), :] + 1).astype(F32)
     width = jnp.sqrt(thermal * mass)
     inverse = 1.0 / mass
@@ -442,20 +542,25 @@
             arrived(ext.at[turn, pl.ds(0, HALO)], r_xh.at[turn - 1, 1])
 
     def all_features(turn):
-        loop(HALO, nb + HALO, lambda n: features(turn, n, True))
-        loop(0, HALO, lambda n: features(turn, n, False))
-        loop(nb + HALO, nb + 2 * HALO, lambda n: features(turn, n, False))
+        features(turn, HALO, nb, True)
+        features(turn, 0, HALO, False)
+        features(turn, nb + HALO, HALO, False)
 
     some = pl.ds(0, nb - 1)
     arrived(xin.at[some], r_in.at[0])
     arrived(pin.at[some], r_in.at[1])
     arrived(nin.at[0, some], r_in.at[2])
+    parts = [component(xin, (), c) for c in range(3)] + [component(pin, (), c) for c in range(3)]
+    parts = times(to_mode, parts)
+    for c in range(6):
+        modes[c] = parts[c]
     gather_force(0)
-    parts = [component(xin, (), c) for c in range(3)] + [
-        component(pin, (), c) + half_step * component(fin, (0,), c) for c in range(3)
-    ]
-    parts = times(to_mode, parts)
-    mode_x, mode_p = drift(0, parts[:3], parts[3:])
+    kicks = times(to_mode, [component(fin, (0,), c) for c in range(3)])
+    mode_x, mode_p = drift(
+        0,
+        [modes[c] for c in range(3)],
+        [modes[3 + c] + half_step * kicks[c] for c in range(3)],
+    )
     spread(xs, (0,), times(to_bead, mode_x))
     send_coords(1)
     for c in range(3):
@@ -464,7 +569,7 @@
 
     gather_coords(1)
     all_features(1)
-    loop(0, nb, lambda i: send_force(1, lax.rem(me + i, nb)))
+    forces(1, nb, lambda i: lax.rem(me + i, nb), send_forces(1))
     arrived(nin.at[1, some], r_in.at[3])
     gather_force(1)
     kicks = times(to_mode, [component(fin, (1,), c) for c in range(3)])
@@ -483,12 +588,13 @@
     all_features(2)
     arrived(pbuf.at[some], r_p)
 
-    def finish(b):
-        for c, f in enumerate(force(2, b)):
-            x_out[c, :, lanes(b)] = ext[2, HALO + b, c]
-            p_out[c, :, lanes(b)] = pbuf[b, c] + half_step * f
-
-    loop(0, nb, finish)
+    def finish(done):
+        for b, parts in done:
+            for c, f in enumerate(parts):
+                x_out[c, :, lanes(b)] = ext[2, HALO + b, c]
+                p_out[c, :, lanes(b)] = pbuf[b, c] + half_step * f
+
+    forces(2, nb, lambda i: i, finish)
 
     arrived(xin.at[some], s_in.at[0])
     arrived(pin.at[some], s_in.at[1])
@@ -529,9 +635,16 @@
                 jax.ShapeDtypeStruct(positions.shape, F32),
                 jax.ShapeDtypeStruct(momenta.shape, F32),
             ),
-            in_specs=[pl.BlockSpec(memory_space=pltpu.SMEM)] + [vmem] * 8,
+            in_specs=[pl.BlockSpec(memory_space=pltpu.SMEM)]
+            + [pl.BlockSpec(memory_space=pltpu.HBM)] * 8,
             out_specs=(vmem, vmem),
             scratch_shapes=[
+                pltpu.VMEM(positions.shape, F32),
+                pltpu.VMEM((nb, LANES), jnp.int32),
+                pltpu.VMEM((2 * HALO + 1, ROWS, LANES), BF16),
+                pltpu.VMEM((nb, nb), F32),
+                pltpu.VMEM((nb, nb), F32),
+                pltpu.VMEM((5, nb, LANES), F32),
                 pltpu.VMEM((nb, *piece), F32),
                 pltpu.VMEM((nb, *piece), F32),
                 pltpu.VMEM((2, nb, *piece), F32),
@@ -558,13 +671,16 @@
                 dma((2, 2)),
                 dma,
                 dma,
+                dma((9,)),
+                pltpu.VMEM((NBR, LANES, LANES), F32),
+                pltpu.VMEM((NBR, LANES, LANES), F32),
             ],
             compiler_params=pltpu.CompilerParams(
-                collective_id=0, has_side_effects=True, vmem_limit_bytes=32 * 1024 * 1024
+                collective_id=0, has_side_effects=True
             ),
             name="path_integral_steps",
         )(
-            neighbours,
+            neighbours.T,
             positions,
             momenta,
             thermal_noise,

time: 94.7 us -> 62.4 us (0.66); the launches traced: 93.3 us -> 62.2 us
  Pallas kernels: 84.9 us -> 59.5 us
  local copies, waits for them, and re-layouts: 7.72 us -> 2.06 us
    pallas_call x1, Pallas kernels: 84.9 us -> 59.5 us  [body(): pl.pallas_call(functools.partial(kernel, nb, ns), out_shape=(jax.ShapeDty...]
    unnamed x19 -> x4, local copies, waits for them, and re-layouts: 7.72 us -> 2.06 us
where the time goes in v2:
time: 62.4 us; the launch traced here: 62.2 us
  Pallas kernels  59.5 us (95%)
  local copies, waits for them, and re-layouts  2.06 us (3%)
  between operations  0.65 us (1%)
    pallas_call x1, Pallas kernels, body(): pl.pallas_call(functools.partial(kernel, nb, ns), out_shape=(jax.ShapeDty...  59.5 us
    unnamed x4, local copies, waits for them, and re-layouts  2.06 us

profile of v2, /device:TPU:1, one launch (start us, length us, event | category | flops | bytes accessed | tf_op | source)
XLA Modules:
  0.0 62.2 jit_solution(14043038115066248260)
XLA Ops:
  0.6 59.5 %path_integral_steps.1 = (f32[3,1,4096]{2,1,0:T(1,128)}, f32[3,1,4096]{2,1,0:T(1,128)}) custom-call(s32[5,32]{1,0:T(8,128)} %bitcast.3, f32[3,1,4096]{2,1,0:T(1,128)} %x_hbm.1, f32[3,1,4096]{2,1,0:T(1,128)} %p_hbm.1, f32[2,3,1,4096]{3,2,1,0:T(1,128)} %noise_hbm.1, s32[32,128]{1,0:T(8,128)} %bitcast.2, bf16[9,48,128]{2,1,0:T(8,128)(2,1)} %constant.8.clone.mult_hbm, ...), custom_call_target="tpu_custom_call" | custom-call | tf_op jit(solution)/shard_map/path_integral_steps/pallas_call | solution.py:632
  60.1 0.0 copy-start
  60.1 1.4 %copy.13 = f32[3,1,4096]{2,1,0:T(1,128)} copy(f32[3,1,4096]{2,1,0:T(1,128)} %get-tuple-element.4) | data formatting | bytes 98304
  61.5 0.0 copy-done
  61.5 0.6 copy.14
Async XLA Ops:
  60.1 1.4 %copy-start = (f32[3,1,4096]{2,1,0:T(1,128)S(1)}, f32[3,1,4096]{2,1,0:T(1,128)}, u32[]{:S(2)}) copy-start(f32[3,1,4096]{2,1,0:T(1,128)} %get-tuple-element.5) | copy-start | bytes 147460

commit v3 on v2

--- a/solution.py
+++ b/solution.py
@@ -16,6 +16,7 @@
 HALO = 4
 NBR = 5
 ROWS = 48
+GROUP = 8
 half_step = 0.025
 time_step = 0.05
 chain_freq = 12.0
@@ -100,8 +101,8 @@
     to_mode,
     to_bead,
     tab_ref,
+    p_ref,
     xin,
-    pin,
     nin,
     ext,
     extq,
@@ -158,6 +159,10 @@
 
         lax.fori_loop(1, nb, step, 0)
 
+    def far_first(i, count, centre):
+        step = lax.div(i + 1, 2)
+        return lax.rem(centre + count // 2 + count + jnp.where(i % 2 == 1, -step, step), count)
+
     def loop(begin, end, body):
         def step(i, carry):
             body(i)
@@ -175,9 +180,8 @@
                 (to_mode_hbm, to_mode),
                 (to_bead_hbm, to_bead),
                 (tab_hbm, tab_ref),
-                (p_hbm.at[:, :, lanes(me)], pin.at[me]),
-                (noise_hbm.at[0, :, :, lanes(me)], nin.at[0, me]),
-                (noise_hbm.at[1, :, :, lanes(me)], nin.at[1, me]),
+                (p_hbm, p_ref),
+                (noise_hbm.at[:, :, :, lanes(me)], nin.at[me]),
             ]
         )
     ]
@@ -216,19 +220,18 @@
     def centred(turn, n):
         return [ext[turn, n, c] - 1.0 for c in range(3)]
 
-    def features(turn, begin, count, own):
-        group = 4
-
-        def several(i):
-            done = [one_features(turn, begin + group * i + k, own) for k in range(group)]
-            for k, (left, heavy, right) in enumerate(done):
-                n = begin + group * i + k
-                fe[n] = left
-                fb[n] = heavy
-                if own:
-                    fa[n - HALO] = right
-
-        loop(0, count // group, several)
+    def features(turn, blocks, own):
+        for n, (left, heavy, right) in [(n, one_features(turn, n, own)) for n in blocks]:
+            fe[n] = left
+            fb[n] = heavy
+            if own:
+                fa[n - HALO] = right
+
+    def own_features(turn):
+        loop(0, nb // 8, lambda i: features(turn, [HALO + 8 * i + k for k in range(8)], True))
+
+    def halo_features(turn):
+        features(turn, [k for k in range(HALO)] + [nb + HALO + k for k in range(HALO)], False)
 
     def one_features(turn, n, own):
         right = None
@@ -304,9 +307,9 @@
         fz = q * (z * plain - sums[2:3])
         return fx, fy, fz
 
-    def forces(turn, count, block_of, take, beside=None):
+    def forces(turn, count, block_of, take):
         squares(block_of(0), even)
-        group = 4 if count % 4 == 0 else 2
+        group = next(g for g in (GROUP, 4, 2) if count % g == 0)
 
         def several(i):
             blocks = [block_of(lax.rem(group * i + k, count)) for k in range(group + 1)]
@@ -316,8 +319,6 @@
                 squares(blocks[k + 1], there)
                 done.append((blocks[k], force(turn, blocks[k], here)))
             take(done)
-            if beside is not None:
-                beside(i)
 
         loop(0, count // group, several)
 
@@ -325,7 +326,10 @@
         def take(done):
             for b, parts in done:
                 for c in range(3):
-                    fout[turn, b, c] = parts[c]
+                    if turn == 0:
+                        fout[0, b, c] = p_ref[c, :, lanes(b)] + half_step * parts[c]
+                    else:
+                        fout[turn, b, c] = parts[c]
 
         return take
 
@@ -366,14 +370,15 @@
             ext[t, nb + HALO : nb + 2 * HALO] = jnp.zeros((HALO, 3, 1, LANES), F32)
         extq[nb + HALO : nb + 2 * HALO] = jnp.zeros((HALO, 1, LANES), F32)
 
-    features(0, HALO, nb, True)
+    own_features(0)
+    staged[6].wait()
     staged[2].wait()
     inner = nb - 2 * HALO
-    early = inner // 6 * 2
+    early = inner // 24 * 8 if inner >= 24 else inner // 6 * 2
     late = inner - early
 
     def inner_block(i):
-        return HALO + lax.rem(me + i, inner)
+        return HALO + far_first(i, inner, jnp.clip(me - HALO, 0, inner - 1))
 
     if early > 0:
         forces(0, early, inner_block, keep_force(0))
@@ -413,30 +418,12 @@
 
     def send_start(t):
         remote(x_hbm.at[:, :, lanes(t)], xin.at[me], s_in.at[0], r_in.at[0], t, dom).start()
-        remote(p_hbm.at[:, :, lanes(t)], pin.at[me], s_in.at[1], r_in.at[1], t, dom).start()
-        remote(noise_hbm.at[0, :, :, lanes(t)], nin.at[0, me], s_in.at[2], r_in.at[2], t, dom).start()
-
-    def send_noise(t):
-        remote(noise_hbm.at[1, :, :, lanes(t)], nin.at[1, me], s_in.at[3], r_in.at[3], t, dom).start()
-
-    rounds = max(late // (4 if late % 4 == 0 else 2), 1)
-    beside = (nb - 1) // rounds if late > 0 else 0
-
-    def send_started(begin, end):
-        loop(begin, end, lambda i: send_start(lax.rem(me + i, nb)))
-
+        remote(noise_hbm.at[:, :, :, lanes(t)], nin.at[me], s_in.at[1], r_in.at[1], t, dom).start()
+
+    others(send_start)
     xin[me] = x_ref[:, :, lanes(me)]
-    send_started(1 + beside * rounds, nb)
     if early > 0:
         loop(0, early, lambda i: send_force(0, inner_block(i)))
-    if late > 0:
-
-        def send_beside(i):
-            for k in range(beside):
-                send_start(lax.rem(me + 1 + beside * i + k, nb))
-
-        forces(0, late, lambda i: inner_block(early + i), send_forces(0), send_beside)
-
     @pl.when(upper)
     def _():
         arrived(ext.at[0, high_halo], r_h.at[0])
@@ -447,18 +434,19 @@
         arrived(ext.at[0, low_halo], r_h.at[2])
         arrived(extq.at[low_halo], r_h.at[3])
 
-    features(0, 0, HALO, False)
-    features(0, nb + HALO, HALO, False)
+    halo_features(0)
 
     def edge(i):
         spot = lax.rem(me + i, 2 * HALO)
         return jnp.where(spot < HALO, spot, spot + inner)
 
     forces(0, 2 * HALO, edge, send_forces(0))
-    others(send_noise)
-
-    for copy in staged[3:]:
-        copy.wait()
+    if late > 0:
+        forces(0, late, lambda i: inner_block(early + i), send_forces(0))
+
+
+    for i in (3, 4, 5, 7):
+        staged[i].wait()
     mass = (types_ref[pl.ds(me, 1), :] + 1).astype(F32)
     width = jnp.sqrt(thermal * mass)
     inverse = 1.0 / mass
@@ -475,7 +463,7 @@
     def drift(turn, mode_x, mode_p):
         next_x, next_p = [], []
         for c in range(3):
-            noise = component(nin, (turn,), c)
+            noise = jnp.concatenate([nin[j, turn, c] for j in range(nb)], axis=0)
             p_new = damping * mode_p[c] + kick * width * noise
             next_x.append(cosine * mode_x[c] + ratio * p_new * inverse)
             next_p.append(cosine * p_new - stiffness * mass * mode_x[c])
@@ -486,52 +474,58 @@
             for j in range(nb):
                 ref[(*lead, j, c)] = parts[c][j : j + 1]
 
+    side = nb // 4
+    own_side = lax.div(me, side)
+    low_owner = jnp.logical_and(lower, me < HALO)
+    high_owner = jnp.logical_and(upper, me >= nb - HALO)
+
     def send_coords(turn):
-        others(
-            lambda t: remote(
+        def inside(t):
+            remote(
                 xs.at[turn - 1, t],
                 ext.at[turn, HALO + me],
                 s_x.at[turn - 1],
-                r_x.at[turn - 1],
+                r_x.at[turn - 1, own_side],
                 t,
                 dom,
             ).start()
-        )
-
-        @pl.when(jnp.logical_and(lower, me < HALO))
-        def _():
-            loop(
-                0,
-                nb,
-                lambda t: remote(
-                    xs.at[turn - 1, lax.rem(me + t, nb)],
-                    ext.at[turn, nb + HALO + me],
-                    s_xh.at[turn - 1],
-                    r_xh.at[turn - 1, 0],
-                    lax.rem(me + t, nb),
-                    dom - 1,
-                ).start(),
+
+        def across(t, slot, which, space):
+            remote(
+                xs.at[turn - 1, t],
+                ext.at[turn, slot],
+                s_xh.at[turn - 1],
+                r_xh.at[turn - 1, which],
+                t,
+                space,
+            ).start()
+
+            @pl.when(t != me)
+            def _():
+                inside(t)
+
+        @pl.when(low_owner)
+        def _():
+            loop(0, nb, lambda i: across(far_first(i, nb, me), nb + HALO + me, 0, dom - 1))
+
+        @pl.when(high_owner)
+        def _():
+            loop(0, nb, lambda i: across(far_first(i, nb, me), me - (nb - HALO), 1, dom + 1))
+
+        @pl.when(jnp.logical_not(jnp.logical_or(low_owner, high_owner)))
+        def _():
+            loop(0, nb - 1, lambda i: inside(far_first(i, nb, me)))
+
+        ext[turn, HALO + me] = xs[turn - 1, me]
+
+    def gather_features(turn):
+        for k in (0, 1, 3, 2):
+            which = lax.rem(own_side + k, 4)
+            arrived(
+                ext.at[turn, pl.ds(0, side - 1 if k == 0 else side)],
+                r_x.at[turn - 1, which],
             )
-
-        @pl.when(jnp.logical_and(upper, me >= nb - HALO))
-        def _():
-            loop(
-                0,
-                nb,
-                lambda t: remote(
-                    xs.at[turn - 1, lax.rem(me + t, nb)],
-                    ext.at[turn, me - (nb - HALO)],
-                    s_xh.at[turn - 1],
-                    r_xh.at[turn - 1, 1],
-                    lax.rem(me + t, nb),
-                    dom + 1,
-                ).start(),
-            )
-
-        ext[turn, HALO + me] = xs[turn - 1, me]
-
-    def gather_coords(turn):
-        arrived(ext.at[turn, pl.ds(0, nb - 1)], r_x.at[turn - 1])
+            features(turn, [HALO + side * which + i for i in range(side)], True)
 
         @pl.when(upper)
         def _():
@@ -541,36 +535,25 @@
         def _():
             arrived(ext.at[turn, pl.ds(0, HALO)], r_xh.at[turn - 1, 1])
 
-    def all_features(turn):
-        features(turn, HALO, nb, True)
-        features(turn, 0, HALO, False)
-        features(turn, nb + HALO, HALO, False)
+        halo_features(turn)
 
     some = pl.ds(0, nb - 1)
     arrived(xin.at[some], r_in.at[0])
-    arrived(pin.at[some], r_in.at[1])
-    arrived(nin.at[0, some], r_in.at[2])
-    parts = [component(xin, (), c) for c in range(3)] + [component(pin, (), c) for c in range(3)]
-    parts = times(to_mode, parts)
-    for c in range(6):
+    arrived(nin.at[some], r_in.at[1])
+    parts = times(to_mode, [component(xin, (), c) for c in range(3)])
+    for c in range(3):
         modes[c] = parts[c]
     gather_force(0)
-    kicks = times(to_mode, [component(fin, (0,), c) for c in range(3)])
-    mode_x, mode_p = drift(
-        0,
-        [modes[c] for c in range(3)],
-        [modes[3 + c] + half_step * kicks[c] for c in range(3)],
-    )
+    kicked = times(to_mode, [component(fin, (0,), c) for c in range(3)])
+    mode_x, mode_p = drift(0, [modes[c] for c in range(3)], kicked)
     spread(xs, (0,), times(to_bead, mode_x))
     send_coords(1)
     for c in range(3):
         modes[c] = mode_x[c]
         modes[3 + c] = mode_p[c]
 
-    gather_coords(1)
-    all_features(1)
-    forces(1, nb, lambda i: lax.rem(me + i, nb), send_forces(1))
-    arrived(nin.at[1, some], r_in.at[3])
+    gather_features(1)
+    forces(1, nb, lambda i: far_first(i, nb, me), send_forces(1))
     gather_force(1)
     kicks = times(to_mode, [component(fin, (1,), c) for c in range(3)])
     mode_x, mode_p = drift(
@@ -584,8 +567,7 @@
     others(lambda t: remote(ps.at[t], pbuf.at[me], s_p, r_p, t, dom).start())
     pbuf[me] = ps[me]
 
-    gather_coords(2)
-    all_features(2)
+    gather_features(2)
     arrived(pbuf.at[some], r_p)
 
     def finish(done):
@@ -597,14 +579,12 @@
     forces(2, nb, lambda i: i, finish)
 
     arrived(xin.at[some], s_in.at[0])
-    arrived(pin.at[some], s_in.at[1])
-    arrived(nin.at[0, some], s_in.at[2])
-    arrived(nin.at[1, some], s_in.at[3])
+    arrived(nin.at[some], s_in.at[1])
     for turn in range(2):
         arrived(fin.at[turn, some], s_f.at[turn])
         arrived(xs.at[turn, some], s_x.at[turn])
 
-        @pl.when(jnp.logical_or(jnp.logical_and(lower, me < HALO), jnp.logical_and(upper, me >= nb - HALO)))
+        @pl.when(jnp.logical_or(low_owner, high_owner))
         def _():
             arrived(xs.at[turn], s_xh.at[turn])
 
@@ -645,9 +625,9 @@
                 pltpu.VMEM((nb, nb), F32),
                 pltpu.VMEM((nb, nb), F32),
                 pltpu.VMEM((5, nb, LANES), F32),
+                pltpu.VMEM(momenta.shape, F32),
                 pltpu.VMEM((nb, *piece), F32),
-                pltpu.VMEM((nb, *piece), F32),
-                pltpu.VMEM((2, nb, *piece), F32),
+                pltpu.VMEM((nb, 2, *piece), F32),
                 pltpu.VMEM((3, nb + 2 * HALO, *piece), F32),
                 pltpu.VMEM((nb + 2 * HALO, 1, LANES), F32),
                 pltpu.VMEM((2, nb, *piece), F32),
@@ -659,19 +639,19 @@
                 pltpu.VMEM((nb + 2 * HALO, LANES, ROWS), BF16),
                 pltpu.VMEM((nb + 2 * HALO, 16, LANES), BF16),
                 pltpu.VMEM((nb, ROWS, LANES), BF16),
-                dma((4,)),
-                dma((4,)),
+                dma((2,)),
+                dma((2,)),
                 dma((4,)),
                 dma((4,)),
                 dma((2,)),
                 dma((2,)),
                 dma((2,)),
-                dma((2,)),
+                dma((2, 4)),
                 dma((2,)),
                 dma((2, 2)),
                 dma,
                 dma,
-                dma((9,)),
+                dma((8,)),
                 pltpu.VMEM((NBR, LANES, LANES), F32),
                 pltpu.VMEM((NBR, LANES, LANES), F32),
             ],

time: 62.4 us -> 60.3 us (0.966); the launches traced: 62.2 us -> 59.3 us
  Pallas kernels: 59.5 us -> 56.6 us
    pallas_call x1, Pallas kernels: 59.5 us -> 56.6 us  [body(): pl.pallas_call(functools.partial(kernel, nb, ns), out_shape=(jax.ShapeDty...]
where the time goes in v3:
time: 60.3 us; the launch traced here: 59.3 us
  Pallas kernels  56.6 us (94%)
  local copies, waits for them, and re-layouts  2.06 us (3%)
  between operations  0.65 us (1%)
    pallas_call x1, Pallas kernels, body(): pl.pallas_call(functools.partial(kernel, nb, ns), out_shape=(jax.ShapeDty...  56.6 us
    unnamed x4, local copies, waits for them, and re-layouts  2.06 us

profile of v3, /device:TPU:1, one launch (start us, length us, event | category | flops | bytes accessed | tf_op | source)
XLA Modules:
  0.0 59.3 jit_solution(16096608388971091211)
XLA Ops:
  0.6 56.6 %path_integral_steps.1 = (f32[3,1,4096]{2,1,0:T(1,128)}, f32[3,1,4096]{2,1,0:T(1,128)}) custom-call(s32[5,32]{1,0:T(8,128)} %bitcast.3, f32[3,1,4096]{2,1,0:T(1,128)} %x_hbm.1, f32[3,1,4096]{2,1,0:T(1,128)} %p_hbm.1, f32[2,3,1,4096]{3,2,1,0:T(1,128)} %noise_hbm.1, s32[32,128]{1,0:T(8,128)} %bitcast.2, bf16[9,48,128]{2,1,0:T(8,128)(2,1)} %constant.8.clone.mult_hbm, ...), custom_call_target="tpu_custom_call" | custom-call | tf_op jit(solution)/shard_map/path_integral_steps/pallas_call | solution.py:612
  57.3 0.0 copy-start
  57.3 1.4 %copy.13 = f32[3,1,4096]{2,1,0:T(1,128)} copy(f32[3,1,4096]{2,1,0:T(1,128)} %get-tuple-element.4) | data formatting | bytes 98304
  58.7 0.0 copy-done
  58.7 0.6 %copy.14 = f32[3,1,4096]{2,1,0:T(1,128)} copy(f32[3,1,4096]{2,1,0:T(1,128)S(1)} %copy-done) | data formatting | bytes 98304
Async XLA Ops:
  57.3 1.4 %copy-start = (f32[3,1,4096]{2,1,0:T(1,128)S(1)}, f32[3,1,4096]{2,1,0:T(1,128)}, u32[]{:S(2)}) copy-start(f32[3,1,4096]{2,1,0:T(1,128)} %get-tuple-element.5) | copy-start | bytes 147460

commit v4 on v3

--- a/solution.py
+++ b/solution.py
@@ -93,8 +93,7 @@
     to_mode_hbm,
     to_bead_hbm,
     tab_hbm,
-    x_out,
-    p_out,
+    both_out,
     x_ref,
     types_ref,
     mult_ref,
@@ -288,13 +287,12 @@
             r = lax.rsqrt(square)
             weight = jnp.exp2((square * r) * (-decay)) * ((r * r) * (r + 0.25))
             high = weight.astype(BF16)
-            low = (weight - high.astype(F32)).astype(BF16)
             left = fb[n]
-            part = jnp.dot(
-                jnp.concatenate([left, left], axis=1),
-                jnp.concatenate([high, low], axis=0),
-                preferred_element_type=F32,
-            )
+            if turn > 0:
+                low = (weight - high.astype(F32)).astype(BF16)
+                left = jnp.concatenate([left, left], axis=1)
+                high = jnp.concatenate([high, low], axis=0)
+            part = jnp.dot(left, high, preferred_element_type=F32)
             total = total + part
             moved = moved + s.astype(F32) * part
         sums = total[0:4] + total[4:8] + total[8:12]
@@ -573,8 +571,8 @@
     def finish(done):
         for b, parts in done:
             for c, f in enumerate(parts):
-                x_out[c, :, lanes(b)] = ext[2, HALO + b, c]
-                p_out[c, :, lanes(b)] = pbuf[b, c] + half_step * f
+                both_out[0, c, :, lanes(b)] = ext[2, HALO + b, c]
+                both_out[1, c, :, lanes(b)] = pbuf[b, c] + half_step * f
 
     forces(2, nb, lambda i: i, finish)
 
@@ -609,15 +607,12 @@
         vmem = pl.BlockSpec(memory_space=pltpu.VMEM)
         piece = (3, 1, LANES)
         dma = pltpu.SemaphoreType.DMA
-        return pl.pallas_call(
+        both = pl.pallas_call(
             functools.partial(kernel, nb, ns),
-            out_shape=(
-                jax.ShapeDtypeStruct(positions.shape, F32),
-                jax.ShapeDtypeStruct(momenta.shape, F32),
-            ),
+            out_shape=jax.ShapeDtypeStruct((2, *positions.shape), F32),
             in_specs=[pl.BlockSpec(memory_space=pltpu.SMEM)]
             + [pl.BlockSpec(memory_space=pltpu.HBM)] * 8,
-            out_specs=(vmem, vmem),
+            out_specs=vmem,
             scratch_shapes=[
                 pltpu.VMEM(positions.shape, F32),
                 pltpu.VMEM((nb, LANES), jnp.int32),
@@ -670,6 +665,7 @@
             jnp.asarray(matrix),
             jnp.asarray(mode_tables(nb)),
         )
+        return both[0], both[1]
 
     spec = P(None, "bead", "space")
     return jax.shard_map(

time: 60.3 us -> 59.3 us (0.983)
    unnamed x4 -> x0, local copies, waits for them, and re-layouts: 2.06 us -> none
    squeeze x0 -> x1, local copies, waits for them, and re-layouts: none -> 1.47 us  [body(): return (both[0], both[1])]
where the time goes in v4:
time: 59.3 us; the launch traced here: 58.2 us
  Pallas kernels  56.1 us (95%)
  local copies, waits for them, and re-layouts  1.47 us (2%)
  between operations  0.64 us (1%)
    pallas_call x1, Pallas kernels, body(): pl.pallas_call(functools.partial(kernel, nb, ns), out_shape=jax.ShapeDtyp...  56.1 us
    squeeze x1, local copies, waits for them, and re-layouts, body(): return (both[0], both[1])  1.47 us

profile of v4, /device:TPU:1, one launch (start us, length us, event | category | flops | bytes accessed | tf_op | source)
XLA Modules:
  0.0 58.2 jit_solution(18394100034112800202)
XLA Ops:
  0.6 56.1 %path_integral_steps.1 = f32[2,3,1,4096]{3,2,1,0:T(1,128)} custom-call(s32[5,32]{1,0:T(8,128)} %bitcast.7, f32[3,1,4096]{2,1,0:T(1,128)} %x_hbm.1, f32[3,1,4096]{2,1,0:T(1,128)} %p_hbm.1, f32[2,3,1,4096]{3,2,1,0:T(1,128)} %noise_hbm.1, s32[32,128]{1,0:T(8,128)} %bitcast.6, bf16[9,48,128]{2,1,0:T(8,128)(2,1)} %constant.8.clone.mult_hbm, ...), custom_call_target="tpu_custom_call" | custom-call | tf_op jit(solution)/shard_map/path_integral_steps/pallas_call | solution.py:610
  56.7 1.5 %slice_bitcast_fusion = (f32[3,1,4096]{2,1,0:T(1,128)}, f32[3,1,4096]{2,1,0:T(1,128)}) fusion(f32[2,3,1,4096]{3,2,1,0:T(1,128)} %path_integral_steps.1), kind=kLoop, calls=%fused_computation | loop fusion | bytes 196608 | tf_op jit(solution)/shard_map/squeeze | solution.py:668
